TPU v7x, 32 devices: a whole 2x2x4 slice. The times are simulated.
32 devices in a mesh: space: 4 (over y, x), batch: 8 (over z, core).
Axes of the slice: x: 2, y: 2, z: 4, core: 2. Of those that a mesh axis runs over, the one named last changes fastest.
Arguments:
- pre_act: bfloat16 [8, 64, 4, 8, 128], P('batch', None, 'space'), may hold values from -6 to 6
- grad_out: bfloat16 [8, 128, 4, 8, 128], P('batch', None, 'space'), may hold values from -6 to 6
- weight: bfloat16 [27, 64, 128], replicated, may hold values from -0.109375 to 0.109375
Outputs:
- grad_in: bfloat16 [8, 64, 4, 8, 128], P('batch', None, 'space')
- weight_grad: float32 [221184], P(('space', 'batch'))
All inputs are finite; a program needn't handle non-finite values.
Results may differ from a plain program's by a relative error of at most 0.001.
Values may be sent and summed in bfloat16 or wider, within the bound.
A program may use at most 64 MiB of HBM per device.

v0:
```python
import jax
import jax.numpy as jnp
from jax import lax
from jax.sharding import PartitionSpec as P

slope = 0.3


def padded(block, sides, width):
    for axis, dim in sides:
        count = lax.axis_size(axis)
        forward = [(i, i + 1) for i in range(count - 1)]
        backward = [(target, source) for source, target in forward]
        low = lax.ppermute(
            lax.slice_in_dim(block, block.shape[dim] - width, None, axis=dim), axis, forward
        )
        high = lax.ppermute(lax.slice_in_dim(block, 0, width, axis=dim), axis, backward)
        block = jnp.concatenate([low, block, high], axis=dim)
    return block


def leaky(values):
    return jnp.where(values > 0, values, slope * values)


def on_device(pre_act, grad_out, weight):
    local_x = pre_act.shape[2]
    local_y = pre_act.shape[3]
    local_z = pre_act.shape[4]
    count = (
        pre_act.shape[0]
        * lax.axis_size("batch")
        * local_x
        * lax.axis_size("space")
        * local_y
        * local_z
    )
    factor = 1.0 / jnp.sqrt(jnp.float32(count))
    act_float = pre_act.astype(jnp.float32)
    yz_pad = ((0, 0), (0, 0), (0, 0), (1, 1), (1, 1))
    grad_hidden = jnp.zeros(pre_act.shape, jnp.float32)
    tap_grads = []
    joined = jnp.concatenate([pre_act, grad_out], axis=1)
    widened = padded(joined, (("space", 2),), 1)
    in_chan = pre_act.shape[1]
    hidden_pad = jnp.pad(
        leaky(widened[:, :in_chan].astype(jnp.float32)).astype(jnp.bfloat16), yz_pad
    )
    grad_pad = jnp.pad(widened[:, in_chan:], yz_pad)
    for tap in range(27):
        shift_x = tap // 9 - 1
        shift_y = tap // 3 % 3 - 1
        shift_z = tap % 3 - 1
        window = grad_pad[
            :,
            :,
            1 - shift_x : 1 - shift_x + local_x,
            1 - shift_y : 1 - shift_y + local_y,
            1 - shift_z : 1 - shift_z + local_z,
        ]
        grad_hidden = grad_hidden + jnp.einsum(
            "ic,scxyz->sixyz", weight[tap], window, preferred_element_type=jnp.float32
        )
        moved = hidden_pad[
            :,
            :,
            1 + shift_x : 1 + shift_x + local_x,
            1 + shift_y : 1 + shift_y + local_y,
            1 + shift_z : 1 + shift_z + local_z,
        ]
        tap_grads.append(
            jnp.einsum("sixyz,scxyz->ic", moved, grad_out, preferred_element_type=jnp.float32)
        )
    grad_in = (grad_hidden * jnp.where(act_float > 0, 1.0, slope)).astype(jnp.bfloat16)
    partial_sum = (jnp.stack(tap_grads) * factor).reshape(-1)
    space_part = lax.psum_scatter(partial_sum, "space", scatter_dimension=0, tiled=True)
    weight_grad = lax.psum_scatter(space_part, "batch", scatter_dimension=0, tiled=True)
    return (grad_in, weight_grad)


def solution(mesh):
    return jax.shard_map(
        on_device,
        mesh=mesh,
        in_specs=(
            P("batch", None, "space", None, None),
            P("batch", None, "space", None, None),
            P(),
        ),
        out_specs=(P("batch", None, "space", None, None), P(("space", "batch"))),
        check_vma=False,
    )
```

profile of v0, /device:TPU:0, one launch (start us, length us, event | category | flops | bytes accessed | tf_op | source)
XLA Modules:
  0.0 161.2 jit_solution(3799746914237049268)
XLA Ops:
  7.2 0.9 copy_dynamic-update-slice_fusion.1
  8.1 1.0 copy_dynamic-update-slice_fusion
  9.2 1.3 collective-permute-start.1
  10.5 5.5 %collective-permute-start = (bf16[1,192,1,8,128]{4,1,3,2,0:T(8,128)(2,1)S(1)}, bf16[1,192,1,8,128]{4,1,3,2,0:T(8,128)(2,1)S(1)}, u32[]{:S(2)}, u32[]{:S(2)}) collective-permute-start(bf16[1,192,1,8,128]{4,1,3,2,0:T(8,128)(2,1)S(1)} %copy_dynamic-update-slice_fusion), channel_id=1, source_target_pairs={{0,8},{8,16},{16,24},{1,9},{9,17},{17,25},{2,10},{10,18},{18,26},{... | collective-permute-start | bytes 1179656 | tf_op jit(solution)/shard_map/ppermute | solution.py:14
  16.0 1.2 dynamic-slice
  17.2 1.2 dynamic-slice.2
  19.8 4.2 %collective-permute-done.1 = bf16[1,192,1,8,128]{4,1,3,2,0:T(8,128)(2,1)S(1)} collective-permute-done((bf16[1,192,1,8,128]{4,1,3,2,0:T(8,128)(2,1)S(1)}, bf16[1,192,1,8,128]{4,1,3,2,0:T(8,128)(2,1)S(1)}, u32[]{:S(2)}, u32[]{:S(2)}) %collective-permute-start.1) | collective-permute-done | bytes 393248 | tf_op jit(solution)/shard_map/ppermute | solution.py:17
  24.0 0.3 collective-permute-done
  24.5 0.9 copy-done.2
  25.6 0.3 fusion.90
  26.1 0.3 convolution_add_fusion.13
  26.4 0.3 convolution_add_fusion.12
  26.6 0.3 convolution_add_fusion.11
  26.9 0.2 fusion.1
  27.1 0.3 convolution_add_fusion.9
  27.4 0.2 convolution_add_fusion.8
  27.6 0.3 convolution_add_fusion.7
  27.8 0.3 convolution_add_fusion.6
  28.3 0.3 convolution_add_fusion.4
  28.6 0.3 convolution_add_fusion.3
  28.9 0.4 copy-done
  29.4 0.3 convolution_add_fusion.1
  29.7 0.3 fusion.14
  30.0 0.3 fusion.12
  30.3 0.3 fusion.11
  30.7 0.3 fusion.9
  31.1 0.2 fusion.42
  31.4 0.2 fusion.41
  31.6 0.2 fusion.40
  31.8 0.2 fusion.39
  32.1 0.2 fusion.38
  32.3 0.2 fusion.37
  32.6 0.2 fusion.36
  32.8 0.2 fusion.35
  33.0 0.3 fusion.34
  33.3 0.2 fusion.33
  33.5 0.2 fusion.32
  33.8 0.2 fusion.31
  34.0 0.2 fusion.30
  34.3 0.2 fusion.29
  34.5 0.2 fusion.28
  34.7 0.2 fusion.27
  35.0 0.2 fusion.26
  35.2 0.3 fusion.25
  35.5 0.2 fusion.24
  35.7 0.2 fusion.23
  35.9 0.2 fusion.22
  36.2 0.2 fusion.21
  36.4 0.2 fusion.20
  36.6 0.2 fusion.19
  36.9 0.2 fusion.18
  37.2 0.2 fusion.17
  37.4 0.2 fusion.16
  37.6 1.1 broadcast_multiply_fusion
  38.8 0.3 fusion.8
  39.1 0.3 convolution_bitcast_fusion.3
  39.3 0.2 fusion.7
  39.5 0.3 fusion.5
  40.0 57.7 %all-reduce.7.cloned.1.call-done = f32[221184]{0:T(1024)} async-done(((f32[221184]{0:T(1024)}), f32[221184]{0:T(1024)}) %all-reduce.7.cloned.1.call-update) | async-done | bytes 884752
  97.7 1.6 %dynamic-slice.1 = f32[55296]{0:T(1024)} dynamic-slice(f32[221184]{0:T(1024)} %all-reduce.7.cloned.1.call-done, u32[]{:T(128)S(6)} %multiply.1), dynamic_slice_sizes={55296} | dynamic-slice | bytes 442372
  99.4 0.3 fusion.15
  99.7 0.7 copy.68
  100.4 52.5 %all-reduce.9.cloned.1.call-done = f32[55296]{0:T(1024)} async-done(((f32[55296]{0:T(1024)}), f32[55296]{0:T(1024)}) %all-reduce.9.cloned.1.call-update) | async-done | bytes 221200
  152.9 1.4 dynamic-slice.3
  (17 shorter events, 1.5 us)
Async XLA Ops:
  7.2 90.6 %all-reduce.7.cloned.1.call-start = ((), (), s32[]{:S(2)}) async-start(), calls=%async_computation | async-start | bytes 1769472
  9.2 14.8 %collective-permute-start.1 = (bf16[1,192,1,8,128]{4,1,3,2,0:T(8,128)(2,1)S(1)}, bf16[1,192,1,8,128]{4,1,3,2,0:T(8,128)(2,1)S(1)}, u32[]{:S(2)}, u32[]{:S(2)}) collective-permute-start(bf16[1,192,1,8,128]{4,1,3,2,0:T(8,128)(2,1)S(1)} %copy_dynamic-update-slice_fusion), channel_id=1, source_target_pairs={{8,0},{16,8},{24,16},{9,1},{17,9},{25,17},{10,2},{18,10},{26,18},{... | collective-permute-start | bytes 1179656 | tf_op jit(solution)/shard_map/ppermute | solution.py:17
  10.5 13.9 %collective-permute-start = (bf16[1,192,1,8,128]{4,1,3,2,0:T(8,128)(2,1)S(1)}, bf16[1,192,1,8,128]{4,1,3,2,0:T(8,128)(2,1)S(1)}, u32[]{:S(2)}, u32[]{:S(2)}) collective-permute-start(bf16[1,192,1,8,128]{4,1,3,2,0:T(8,128)(2,1)S(1)} %copy_dynamic-update-slice_fusion), channel_id=1, source_target_pairs={{0,8},{8,16},{16,24},{1,9},{9,17},{17,25},{2,10},{10,18},{18,26},{... | collective-permute-start | bytes 1179656 | tf_op jit(solution)/shard_map/ppermute | solution.py:14
  24.5 1.0 copy-start.2
  28.3 1.0 copy-start
  38.7 114.2 %all-reduce.9.cloned.1.call-start = ((), (), s32[]{:S(2)}) async-start(), calls=%async_computation.1 | async-start | bytes 442368
  39.8 59.6 %copy-start.1 = (bf16[1,64,1,8,128]{4,3,2,1,0:T(8,128)(2,1)S(1)}, bf16[1,64,1,8,128]{4,3,2,1,0:T(8,128)(2,1)}, u32[]{:S(2)}) copy-start(bf16[1,64,1,8,128]{4,3,2,1,0:T(8,128)(2,1)} %param.3) | copy-start | bytes 393220
Sparse Core Ops, SparseCore 0:
  38.8 58.8 all-reduce.6
  100.1 52.8 all-reduce.8
where the time goes:
time: 162 us; the launch traced here: 161 us
  waiting for transfers between devices  115 us (71%)
  between operations  15.8 us (10%)
  matrix products  12.7 us (8%)
  local copies, waits for them, and re-layouts  9.64 us (6%)
  starting transfers between devices  6.89 us (4%)
    unnamed x4, waiting for transfers between devices  110 us
    unnamed x12, local copies, waits for them, and re-layouts  8.57 us
    dot_general x27, matrix products, on_device(): jnp.einsum('ic,scxyz->sixyz', weight[tap], window, preferred_element_type...  6.4 us
    dot_general x27, matrix products, on_device(): jnp.einsum('sixyz,scxyz->ic', moved, grad_out, preferred_element_type=jnp...  6.29 us
    ppermute x1, starting transfers between devices, padded(): lax.ppermute(lax.slice_in_dim(block, block.shape[dim] - width, None, axis...  5.52 us
    ppermute x1, waiting for transfers between devices, padded(): lax.ppermute(lax.slice_in_dim(block, 0, width, axis=dim), axis, backward)  4.22 us
  transfers between devices with their start and end apart: 4, of which 4 were waited for; matrix products, arithmetic and copies ran while one was open for 3% of the time, Pallas kernels for 0%

commit v1 on v0

--- a/solution.py
+++ b/solution.py
@@ -1,6 +1,10 @@
+import functools
+
 import jax
 import jax.numpy as jnp
 from jax import lax
+from jax.experimental import pallas as pl
+from jax.experimental.pallas import tpu as pltpu
 from jax.sharding import PartitionSpec as P
 
 slope = 0.3
@@ -78,9 +82,314 @@
     return (grad_in, weight_grad)
 
 
+MESH = pl.DeviceIdType.MESH
+
+
+def prepare(values, scratch, target):
+    channels, rows, lanes = values.shape
+    scratch[0 : channels * rows, :] = values.reshape(channels * rows, lanes)
+    lane = lax.broadcasted_iota(jnp.int32, (channels, lanes), 1)
+    blank = jnp.zeros((3 * channels, lanes), target.dtype)
+    target[:, 0:lanes] = blank
+    target[:, (rows + 1) * lanes : (rows + 2) * lanes] = blank
+    for row in range(rows):
+        block = scratch[pl.ds(row, channels, stride=rows), :]
+        before = jnp.where(lane == 0, 0.0, pltpu.roll(block, 1, 1))
+        after = jnp.where(lane == lanes - 1, 0.0, pltpu.roll(block, lanes - 1, 1))
+        for place, shifted in enumerate((before, block, after)):
+            target[
+                place * channels : (place + 1) * channels, (row + 1) * lanes : (row + 2) * lanes
+            ] = shifted.astype(target.dtype)
+
+
+def kernel(
+    sizes,
+    factor,
+    scatter,
+    pre_ref,
+    grad_ref,
+    weight_hbm,
+    grad_in_ref,
+    weight_grad_ref,
+    pre_halo,
+    grad_halo,
+    weight_ref,
+    plane,
+    hidden_rows,
+    grad_rows,
+    total,
+    partial,
+    halo_send,
+    halo_recv,
+    weight_sem,
+    *stage_refs,
+):
+    space_count, batch_count = sizes
+    space, batch = lax.axis_index("space"), lax.axis_index("batch")
+    channels, rows, lanes = pre_ref.shape
+    cells = rows * lanes
+
+    coords = dict(c=lax.rem(batch, 2), z=batch // 2, x=lax.rem(space, 2), y=space // 2)
+    extents = dict(c=2, z=batch_count // 2, x=2, y=space_count // 2)
+
+    def peer(axis, place):
+        moved = dict(coords, **{axis: place})
+        return (moved["y"] * 2 + moved["x"], moved["z"] * 2 + moved["c"])
+
+    weight_copy = pltpu.make_async_copy(weight_hbm, weight_ref, weight_sem)
+    weight_copy.start()
+
+    has_left, has_right = space > 0, space < space_count - 1
+    barrier = pltpu.get_barrier_semaphore()
+    for there, condition in ((space - 1, has_left), (space + 1, has_right)):
+
+        @pl.when(condition)
+        def _():
+            pl.semaphore_signal(barrier, inc=1, device_id=(there, batch), device_id_type=MESH)
+
+    greeted = 0
+    if scatter:
+        for axis, extent in extents.items():
+            for step in range(1, extent):
+                pl.semaphore_signal(
+                    barrier,
+                    inc=1,
+                    device_id=peer(axis, lax.rem(coords[axis] + step, extent)),
+                    device_id_type=MESH,
+                )
+                greeted += 1
+    beside = jnp.where(has_left, 1, 0) + jnp.where(has_right, 1, 0)
+    pl.semaphore_wait(barrier, greeted + beside)
+
+    def halo(source, slots, index, slot):
+        there = space + 1 if slot == 0 else space - 1
+        return pltpu.make_async_remote_copy(
+            src_ref=source,
+            dst_ref=slots.at[slot],
+            send_sem=halo_send.at[index, slot],
+            recv_sem=halo_recv.at[index, slot],
+            device_id=(there, batch),
+            device_id_type=MESH,
+        )
+
+    pairs = ((pre_ref, pre_halo), (grad_ref, grad_halo))
+    for index, (source, slots) in enumerate(pairs):
+        for slot, condition in ((0, has_right), (1, has_left)):
+
+            @pl.when(condition)
+            def _():
+                halo(source, slots, index, slot).start()
+
+    def arrive(index):
+        source, slots = pairs[index]
+        for slot, condition in ((0, has_left), (1, has_right)):
+
+            @pl.when(condition)
+            def _():
+                halo(source, slots, index, slot).wait_recv()
+
+            @pl.when(jnp.logical_not(condition))
+            def _():
+                slots[slot] = jnp.zeros(slots.shape[1:], slots.dtype)
+
+    def hidden_plane(values, shift):
+        prepare(leaky(values.astype(jnp.float32)), plane, hidden_rows.at[shift + 1])
+
+    def grad_plane(values, shift):
+        prepare(values.astype(jnp.float32), plane, grad_rows.at[shift + 1])
+
+    out_chan = grad_ref.shape[0]
+
+    def weight_terms(shift_x):
+        own = grad_rows[1, out_chan : 2 * out_chan, lanes : lanes + cells]
+        for shift_y in (-1, 0, 1):
+            start = (9 * (shift_x + 1) + 3 * (shift_y + 1)) * channels
+            term = lax.dot_general(
+                hidden_rows[shift_x + 1, :, (1 + shift_y) * lanes : (1 + shift_y) * lanes + cells],
+                own,
+                (((1,), (1,)), ((), ())),
+                preferred_element_type=jnp.float32,
+            )
+            partial[start : start + 3 * channels, :] = term * factor
+
+    def input_terms(shift_x, first):
+        for shift_y in (-1, 0, 1):
+            tap = 9 * (shift_x + 1) + 3 * (shift_y + 1)
+            term = jnp.dot(
+                jnp.concatenate([weight_ref[tap + 2], weight_ref[tap + 1], weight_ref[tap]], axis=1),
+                grad_rows[1 - shift_x, :, (1 - shift_y) * lanes : (1 - shift_y) * lanes + cells],
+                preferred_element_type=jnp.float32,
+            )
+            if first and shift_y == -1:
+                total[...] = term
+            else:
+                total[...] += term
+
+    grad_plane(grad_ref[...], 0)
+    hidden_plane(pre_ref[...], 0)
+    weight_terms(0)
+    arrive(0)
+    hidden_plane(pre_halo[0], -1)
+    hidden_plane(pre_halo[1], 1)
+    weight_terms(-1)
+    weight_terms(1)
+
+    def finish_input():
+        arrive(1)
+        grad_plane(grad_halo[0], -1)
+        grad_plane(grad_halo[1], 1)
+        input_terms(-1, False)
+        input_terms(1, False)
+        for row in range(rows):
+            plane[pl.ds(row, channels, stride=rows), :] = total[:, row * lanes : (row + 1) * lanes]
+        back = plane[0 : channels * rows, :].reshape(channels, rows, lanes)
+        act = pre_ref[...].astype(jnp.float32)
+        grad_in_ref[...] = (back * jnp.where(act > 0, 1.0, slope)).astype(grad_in_ref.dtype)
+
+    def own_input():
+        weight_copy.wait()
+        input_terms(0, True)
+
+    if scatter:
+        held, stages = stage_refs[0], stage_refs[1:]
+        piece = partial.shape[0] // 8 * 8 - 8
+        piece = piece // (space_count * batch_count)
+        padded_piece = held.shape[-2]
+        partial[partial.shape[0] - 8 :, :] = jnp.zeros((8, lanes), jnp.float32)
+        for s in range(space_count):
+            for b in range(batch_count):
+                start = (s * batch_count + b) * piece
+                held[b % 2, s // 2, b // 2, s % 2] = partial[start : start + padded_piece, :]
+        waiting = []
+        for number, axis in enumerate("cyzx"):
+            received, summed, send_sem, recv_sem = stages[4 * number : 4 * number + 4]
+            extent, mine = extents[axis], coords[axis]
+            copies = []
+            for step in range(1, extent):
+                place = lax.rem(mine + step, extent)
+                copy = pltpu.make_async_remote_copy(
+                    src_ref=held.at[place],
+                    dst_ref=received.at[step - 1],
+                    send_sem=send_sem.at[step - 1],
+                    recv_sem=recv_sem.at[step - 1],
+                    device_id=peer(axis, place),
+                    device_id_type=MESH,
+                )
+                copy.start()
+                copies.append(copy)
+            if axis == "c":
+                own_input()
+            if axis == "x":
+                finish_input()
+            value = held[mine]
+            for step, copy in enumerate(copies):
+                copy.wait_recv()
+                value = value + received[step]
+            waiting += copies
+            if axis == "x":
+                weight_grad_ref[...] = value
+            else:
+                summed[...] = value
+                held = summed
+        for copy in waiting:
+            copy.wait_send()
+    else:
+        own_input()
+        finish_input()
+        weight_grad_ref[...] = partial[...]
+
+    for index, (source, slots) in enumerate(pairs):
+        for slot, condition in ((0, has_right), (1, has_left)):
+
+            @pl.when(condition)
+            def _():
+                halo(source, slots, index, slot).wait_send()
+
+
+def fused_device(pre_act, grad_out, weight):
+    samples, channels, local_x, rows, lanes = pre_act.shape
+    out_chan, taps = grad_out.shape[1], weight.shape[0]
+    space_count, batch_count = lax.axis_size("space"), lax.axis_size("batch")
+    fits = (
+        samples == 1
+        and local_x == 1
+        and taps == 27
+        and rows == 8
+        and lanes == 128
+        and out_chan == 128
+        and channels % 16 == 0
+        and space_count > 1
+    )
+    if not fits:
+        return on_device(pre_act, grad_out, weight)
+    count = samples * batch_count * local_x * space_count * rows * lanes
+    factor = 1.0 / count**0.5
+    devices = space_count * batch_count
+    total_rows = taps * channels
+    scatter = (
+        space_count % 2 == 0 and batch_count % 2 == 0 and total_rows % devices == 0
+    )
+    cells = rows * lanes
+    widest = max(channels, out_chan)
+    bf16, f32 = jnp.bfloat16, jnp.float32
+    scratch = [
+        pltpu.VMEM((2, channels, rows, lanes), bf16),
+        pltpu.VMEM((2, out_chan, rows, lanes), bf16),
+        pltpu.VMEM((taps, channels, out_chan), bf16),
+        pltpu.VMEM((widest * rows, lanes), f32),
+        pltpu.VMEM((3, 3 * channels, cells + 2 * lanes), bf16),
+        pltpu.VMEM((3, 3 * out_chan, cells + 2 * lanes), bf16),
+        pltpu.VMEM((channels, cells), f32),
+        pltpu.VMEM((total_rows + 8 if scatter else total_rows, out_chan), f32),
+        pltpu.SemaphoreType.DMA((2, 2)),
+        pltpu.SemaphoreType.DMA((2, 2)),
+        pltpu.SemaphoreType.DMA,
+    ]
+    owned = total_rows
+    if scatter:
+        piece = total_rows // devices
+        owned = -(-piece // 8) * 8
+        sizes = [2, space_count // 2, batch_count // 2, 2]
+        tile = (owned, out_chan)
+        scratch.append(pltpu.VMEM((*sizes, *tile), f32))
+        for number, extent in enumerate(sizes):
+            rest = (*sizes[number + 1 :], *tile)
+            scratch += [
+                pltpu.VMEM((max(extent - 1, 1), *rest), f32),
+                pltpu.VMEM(rest, f32),
+                pltpu.SemaphoreType.DMA((max(extent - 1, 1),)),
+                pltpu.SemaphoreType.DMA((max(extent - 1, 1),)),
+            ]
+    vmem = pl.BlockSpec(memory_space=pltpu.VMEM)
+    grad_in, weight_grad = pl.pallas_call(
+        functools.partial(kernel, (space_count, batch_count), factor, scatter),
+        out_shape=(
+            jax.ShapeDtypeStruct((channels, rows, lanes), bf16),
+            jax.ShapeDtypeStruct((owned, out_chan), f32),
+        ),
+        in_specs=[vmem, vmem, pl.BlockSpec(memory_space=pl.ANY)],
+        out_specs=(vmem, vmem),
+        scratch_shapes=scratch,
+        compiler_params=pltpu.CompilerParams(
+            collective_id=0, has_side_effects=True, vmem_limit_bytes=48 * 2**20
+        ),
+    )(
+        pre_act.reshape(channels, rows, lanes),
+        grad_out.reshape(out_chan, rows, lanes),
+        weight,
+    )
+    grad_in = grad_in.reshape(pre_act.shape)
+    if scatter:
+        return grad_in, weight_grad[:piece].reshape(-1)
+    space_part = lax.psum_scatter(
+        weight_grad.reshape(-1), "space", scatter_dimension=0, tiled=True
+    )
+    return grad_in, lax.psum_scatter(space_part, "batch", scatter_dimension=0, tiled=True)
+
+
 def solution(mesh):
     return jax.shard_map(
-        on_device,
+        fused_device,
         mesh=mesh,
         in_specs=(
             P("batch", None, "space", None, None),

time: 162 us -> 40.1 us (0.25)
  waiting for transfers between devices: 115 us -> 0 us
  Pallas kernels: 0 us -> 35.1 us
  between operations: 15.8 us -> 0.65 us
  matrix products: 12.7 us -> 0 us
  starting transfers between devices: 6.89 us -> 0 us
  local copies, waits for them, and re-layouts: 9.64 us -> 4.13 us
    unnamed x4 -> x0, waiting for transfers between devices: 110 us -> none
    pallas_call x0 -> x1, Pallas kernels: none -> 35.1 us  [fused_device(): pl.pallas_call(functools.partial(kernel, (space_count, batch_count), fact...]
    dot_general x54 -> x0, matrix products: 12.7 us -> none  [the longest x27 6.4 us: on_device(): jnp.einsum('ic,scxyz->sixyz', weight[tap], window, preferred_element_type...]
    ppermute x2 -> x0, starting transfers between devices: 6.82 us -> none  [the longest x1 5.52 us: padded(): lax.ppermute(lax.slice_in_dim(block, block.shape[dim] - width, None, axis...]
    unnamed x12 -> x7, local copies, waits for them, and re-layouts: 8.57 us -> 3.51 us
    ppermute x2 -> x0, waiting for transfers between devices: 4.55 us -> none  [the longest x1 4.22 us: padded(): lax.ppermute(lax.slice_in_dim(block, 0, width, axis=dim), axis, backward)]
  transfers between devices with their start and end apart: 4 -> 0, of which waited for: 4 -> 0; matrix products, arithmetic and copies ran while one was open for 3% -> 0% of each run, Pallas kernels for 0% -> 0%
where the time goes in v1:
time: 40.1 us; the launch traced here: 39.9 us
  Pallas kernels  35.1 us (88%)
  local copies, waits for them, and re-layouts  4.13 us (10%)
  between operations  0.65 us (2%)
    pallas_call x1, Pallas kernels, fused_device(): pl.pallas_call(functools.partial(kernel, (space_count, batch_count), fact...  35.1 us
    unnamed x7, local copies, waits for them, and re-layouts  3.51 us

profile of v1, /device:TPU:0, one launch (start us, length us, event | category | flops | bytes accessed | tf_op | source)
XLA Modules:
  0.0 39.9 jit_solution(2880343559062097947)
XLA Ops:
  0.6 0.0 copy-start
  0.6 1.0 %copy-done = bf16[27,64,128]{2,1,0:T(8,128)(2,1)S(1)} copy-done((bf16[27,64,128]{2,1,0:T(8,128)(2,1)S(1)}, bf16[27,64,128]{2,1,0:T(8,128)(2,1)}, u32[]{:S(2)}) %copy-start) | copy-done | bytes 442392
  1.6 0.0 copy-start.1
  1.6 0.9 %copy-done.1 = bf16[1,128,1,8,128]{4,3,2,1,0:T(8,128)(2,1)S(1)} copy-done((bf16[1,128,1,8,128]{4,3,2,1,0:T(8,128)(2,1)S(1)}, bf16[1,128,1,8,128]{4,3,2,1,0:T(8,128)(2,1)}, u32[]{:S(2)}) %copy-start.1) | copy-done | bytes 262168
  2.6 0.0 copy-start.2
  2.6 0.9 %copy-done.2 = bf16[1,64,1,8,128]{4,3,2,1,0:T(8,128)(2,1)S(1)} copy-done((bf16[1,64,1,8,128]{4,3,2,1,0:T(8,128)(2,1)S(1)}, bf16[1,64,1,8,128]{4,3,2,1,0:T(8,128)(2,1)}, u32[]{:S(2)}) %copy-start.2) | copy-done | bytes 131096
  3.5 35.1 %shard_map.50 = (bf16[64,8,128]{2,1,0:T(8,128)(2,1)S(1)}, f32[56,128]{1,0:T(8,128)S(1)}) custom-call(bf16[64,8,128]{2,1,0:T(8,128)(2,1)S(1)} %bitcast.8, bf16[128,8,128]{2,1,0:T(8,128)(2,1)S(1)} %bitcast.7, bf16[27,64,128]{2,1,0:T(8,128)(2,1)S(1)} %copy-done), custom_call_target="tpu_custom_call" | custom-call | tf_op jit(solution)/shard_map/pallas_call | solution.py:364
  38.6 0.6 %slice_bitcast_fusion = f32[6912]{0:T(1024)} fusion(f32[56,128]{1,0:T(8,128)S(1)} %get-tuple-element.5), kind=kLoop, calls=%fused_computation | loop fusion | bytes 55296 | tf_op jit(solution)/shard_map/reshape | solution.py:383
  39.2 0.7 %copy.7 = bf16[1,64,1,8,128]{4,3,2,1,0:T(8,128)(2,1)} copy(bf16[1,64,1,8,128]{4,3,2,1,0:T(8,128)(2,1)S(1)} %bitcast.9) | data formatting | bytes 262144
Async XLA Ops:
  0.6 1.0 %copy-start = (bf16[27,64,128]{2,1,0:T(8,128)(2,1)S(1)}, bf16[27,64,128]{2,1,0:T(8,128)(2,1)}, u32[]{:S(2)}) copy-start(bf16[27,64,128]{2,1,0:T(8,128)(2,1)} %weight_hbm.1) | copy-start | bytes 1327108
  1.6 0.9 %copy-start.1 = (bf16[1,128,1,8,128]{4,3,2,1,0:T(8,128)(2,1)S(1)}, bf16[1,128,1,8,128]{4,3,2,1,0:T(8,128)(2,1)}, u32[]{:S(2)}) copy-start(bf16[1,128,1,8,128]{4,3,2,1,0:T(8,128)(2,1)} %param.4) | copy-start | bytes 786436
  2.6 0.9 %copy-start.2 = (bf16[1,64,1,8,128]{4,3,2,1,0:T(8,128)(2,1)S(1)}, bf16[1,64,1,8,128]{4,3,2,1,0:T(8,128)(2,1)}, u32[]{:S(2)}) copy-start(bf16[1,64,1,8,128]{4,3,2,1,0:T(8,128)(2,1)} %param.3) | copy-start | bytes 393220

commit v2 on v1

v2 whole, which is shorter than its diff:
```python
import functools

import jax
import jax.numpy as jnp
from jax import lax
from jax.experimental import pallas as pl
from jax.experimental.pallas import tpu as pltpu
from jax.sharding import PartitionSpec as P

slope = 0.3


def padded(block, sides, width):
    for axis, dim in sides:
        count = lax.axis_size(axis)
        forward = [(i, i + 1) for i in range(count - 1)]
        backward = [(target, source) for source, target in forward]
        low = lax.ppermute(
            lax.slice_in_dim(block, block.shape[dim] - width, None, axis=dim), axis, forward
        )
        high = lax.ppermute(lax.slice_in_dim(block, 0, width, axis=dim), axis, backward)
        block = jnp.concatenate([low, block, high], axis=dim)
    return block


def leaky(values):
    return jnp.where(values > 0, values, slope * values)


def on_device(pre_act, grad_out, weight):
    local_x = pre_act.shape[2]
    local_y = pre_act.shape[3]
    local_z = pre_act.shape[4]
    count = (
        pre_act.shape[0]
        * lax.axis_size("batch")
        * local_x
        * lax.axis_size("space")
        * local_y
        * local_z
    )
    factor = 1.0 / jnp.sqrt(jnp.float32(count))
    act_float = pre_act.astype(jnp.float32)
    yz_pad = ((0, 0), (0, 0), (0, 0), (1, 1), (1, 1))
    grad_hidden = jnp.zeros(pre_act.shape, jnp.float32)
    tap_grads = []
    joined = jnp.concatenate([pre_act, grad_out], axis=1)
    widened = padded(joined, (("space", 2),), 1)
    in_chan = pre_act.shape[1]
    hidden_pad = jnp.pad(
        leaky(widened[:, :in_chan].astype(jnp.float32)).astype(jnp.bfloat16), yz_pad
    )
    grad_pad = jnp.pad(widened[:, in_chan:], yz_pad)
    for tap in range(27):
        shift_x = tap // 9 - 1
        shift_y = tap // 3 % 3 - 1
        shift_z = tap % 3 - 1
        window = grad_pad[
            :,
            :,
            1 - shift_x : 1 - shift_x + local_x,
            1 - shift_y : 1 - shift_y + local_y,
            1 - shift_z : 1 - shift_z + local_z,
        ]
        grad_hidden = grad_hidden + jnp.einsum(
            "ic,scxyz->sixyz", weight[tap], window, preferred_element_type=jnp.float32
        )
        moved = hidden_pad[
            :,
            :,
            1 + shift_x : 1 + shift_x + local_x,
            1 + shift_y : 1 + shift_y + local_y,
            1 + shift_z : 1 + shift_z + local_z,
        ]
        tap_grads.append(
            jnp.einsum("sixyz,scxyz->ic", moved, grad_out, preferred_element_type=jnp.float32)
        )
    grad_in = (grad_hidden * jnp.where(act_float > 0, 1.0, slope)).astype(jnp.bfloat16)
    partial_sum = (jnp.stack(tap_grads) * factor).reshape(-1)
    space_part = lax.psum_scatter(partial_sum, "space", scatter_dimension=0, tiled=True)
    weight_grad = lax.psum_scatter(space_part, "batch", scatter_dimension=0, tiled=True)
    return (grad_in, weight_grad)


MESH = pl.DeviceIdType.MESH


def prepare(values, scratch, target):
    channels, rows, lanes = values.shape
    scratch[0 : channels * rows, :] = values.reshape(channels * rows, lanes)
    lane = lax.broadcasted_iota(jnp.int32, (channels, lanes), 1)
    blank = jnp.zeros((3 * channels, lanes), target.dtype)
    target[:, 0:lanes] = blank
    target[:, (rows + 1) * lanes : (rows + 2) * lanes] = blank
    for row in range(rows):
        block = scratch[pl.ds(row, channels, stride=rows), :]
        before = jnp.where(lane == 0, 0.0, pltpu.roll(block, 1, 1))
        after = jnp.where(lane == lanes - 1, 0.0, pltpu.roll(block, lanes - 1, 1))
        for place, shifted in enumerate((before, block, after)):
            target[
                place * channels : (place + 1) * channels, (row + 1) * lanes : (row + 2) * lanes
            ] = shifted.astype(target.dtype)


def kernel(
    sizes,
    factor,
    scatter,
    pre_hbm,
    grad_hbm,
    weight_hbm,
    grad_in_ref,
    weight_grad_ref,
    pre_ref,
    grad_ref,
    weight_ref,
    pre_halo,
    grad_halo,
    plane,
    hidden_rows,
    grad_rows,
    total,
    partial,
    local_sem,
    direct_send,
    direct_recv,
    passed_send,
    passed_recv,
    *stage_refs,
):
    space_count, batch_count = sizes
    space, batch = lax.axis_index("space"), lax.axis_index("batch")
    channels, rows, lanes = pre_ref.shape
    out_chan = grad_ref.shape[0]
    cells = rows * lanes

    coords = dict(c=lax.rem(batch, 2), z=batch // 2, x=lax.rem(space, 2), y=space // 2)
    extents = dict(c=2, z=batch_count // 2, x=2, y=space_count // 2)
    side = coords["x"]

    def peer(axis, place):
        moved = dict(coords, **{axis: place})
        return (moved["y"] * 2 + moved["x"], moved["z"] * 2 + moved["c"])

    local = [
        pltpu.make_async_copy(source, target, local_sem.at[place])
        for place, (source, target) in enumerate(
            ((grad_hbm, grad_ref), (pre_hbm, pre_ref), (weight_hbm, weight_ref))
        )
    ]
    for copy in local:
        copy.start()

    barrier = pltpu.get_barrier_semaphore()
    low, high = space >= 2, space < space_count - 2
    if scatter:
        greeted = 0
        for axis, extent in extents.items():
            for step in range(1, extent):
                pl.semaphore_signal(
                    barrier,
                    inc=1,
                    device_id=peer(axis, lax.rem(coords[axis] + step, extent)),
                    device_id_type=MESH,
                )
                greeted += 1
        pl.semaphore_wait(barrier, greeted)
    else:
        pl.semaphore_signal(
            barrier, inc=1, device_id=peer("x", 1 - side), device_id_type=MESH
        )
        for there, condition in ((space - 2, low), (space + 2, high)):

            @pl.when(condition)
            def _():
                pl.semaphore_signal(barrier, inc=1, device_id=(there, batch), device_id_type=MESH)

        pl.semaphore_wait(barrier, 1 + jnp.where(low, 1, 0) + jnp.where(high, 1, 0))

    half = out_chan // 2
    messages = [
        (pre_hbm, lambda slot: pre_halo.at[slot]),
        (grad_hbm.at[0:half], lambda slot: grad_halo.at[slot, 0:half]),
        (grad_hbm.at[half:out_chan], lambda slot: grad_halo.at[slot, half:out_chan]),
    ]
    near = 1 - side
    passes = jnp.where(side == 0, space < space_count - 2, space >= 2)
    gets = jnp.where(side == 0, space >= 2, space < space_count - 2)
    beyond = jnp.where(side == 0, space + 2, space - 2)

    def direct(index):
        source, slots = messages[index]
        return pltpu.make_async_remote_copy(
            src_ref=source,
            dst_ref=slots(side),
            send_sem=direct_send.at[index],
            recv_sem=direct_recv.at[index],
            device_id=peer("x", 1 - side),
            device_id_type=MESH,
        )

    def passed(index):
        slots = messages[index][1]
        return pltpu.make_async_remote_copy(
            src_ref=slots(near),
            dst_ref=slots(side),
            send_sem=passed_send.at[index],
            recv_sem=passed_recv.at[index],
            device_id=(beyond, batch),
            device_id_type=MESH,
        )

    sent = [direct(index) for index in range(3)]
    for copy in sent:
        copy.start()

    def pass_on(index):
        sent[index].wait_recv()

        @pl.when(passes)
        def _():
            passed(index).start()

    def take(index, target):
        @pl.when(gets)
        def _():
            passed(index).wait_recv()

        @pl.when(jnp.logical_not(gets))
        def _():
            target[side] = jnp.zeros(target.shape[1:], target.dtype)

    def hidden_plane(values, place):
        prepare(leaky(values.astype(jnp.float32)), plane, hidden_rows.at[place])

    def grad_plane(values, place):
        prepare(values.astype(jnp.float32), plane, grad_rows.at[place])

    def weight_terms(place):
        own = grad_rows[1, out_chan : 2 * out_chan, lanes : lanes + cells]
        for shift_y in (-1, 0, 1):
            start = (9 * place + 3 * (shift_y + 1)) * channels
            if not isinstance(place, int):
                start = pl.multiple_of(start, 8)
            term = lax.dot_general(
                hidden_rows[place, :, (1 + shift_y) * lanes : (1 + shift_y) * lanes + cells],
                own,
                (((1,), (1,)), ((), ())),
                preferred_element_type=jnp.float32,
            )
            partial[pl.ds(start, 3 * channels), :] = term * factor

    def input_terms(place, first):
        for shift_y in (-1, 0, 1):
            tap = 9 * (2 - place) + 3 * (shift_y + 1)
            term = jnp.dot(
                jnp.concatenate([weight_ref[tap + 2], weight_ref[tap + 1], weight_ref[tap]], axis=1),
                grad_rows[place, :, (1 - shift_y) * lanes : (1 - shift_y) * lanes + cells],
                preferred_element_type=jnp.float32,
            )
            if first and shift_y == -1:
                total[...] = term
            else:
                total[...] += term

    near_place, far_place = 2 * near, 2 * side

    local[0].wait()
    local[1].wait()
    grad_plane(grad_ref[...], 1)
    hidden_plane(pre_ref[...], 1)
    pass_on(0)
    weight_terms(1)
    hidden_plane(pre_halo[near], near_place)
    weight_terms(near_place)
    local[2].wait()
    pass_on(1)
    take(0, pre_halo)
    hidden_plane(pre_halo[side], far_place)
    weight_terms(far_place)

    def near_input():
        grad_plane(grad_halo[near], near_place)
        input_terms(near_place, False)

    def far_input():
        @pl.when(gets)
        def _():
            passed(1).wait_recv()

        take(2, grad_halo)
        grad_plane(grad_halo[side], far_place)
        input_terms(far_place, False)
        for row in range(rows):
            plane[pl.ds(row, channels, stride=rows), :] = total[:, row * lanes : (row + 1) * lanes]
        back = plane[0 : channels * rows, :].reshape(channels, rows, lanes)
        act = pre_ref[...].astype(jnp.float32)
        grad_in_ref[...] = (back * jnp.where(act > 0, 1.0, slope)).astype(grad_in_ref.dtype)

    waiting = list(sent)
    if scatter:
        held, stages = stage_refs[0], stage_refs[1:]
        padded_piece = held.shape[-2]
        piece = (partial.shape[0] - 8) // (space_count * batch_count)
        partial[partial.shape[0] - 8 :, :] = jnp.zeros((8, lanes), jnp.float32)

        def pack(chunk):
            for y in range(extents["y"]):
                for b in range(batch_count):
                    start = ((2 * y + chunk) * batch_count + b) * piece
                    held[b % 2, chunk, y, b // 2] = partial[start : start + padded_piece, :]

        def refs(axis):
            number = "cyzx".index(axis)
            return stages[4 * number : 4 * number + 4]

        def begin(axis, chunk):
            received, _, send_sem, recv_sem = refs(axis)
            copies = []
            for step in range(1, extents[axis]):
                place = lax.rem(coords[axis] + step, extents[axis])
                if axis == "c":
                    source = held.at[place, chunk]
                else:
                    source = refs("cyz"["cyz".index(axis) - 1])[1].at[chunk, place]
                copy = pltpu.make_async_remote_copy(
                    src_ref=source,
                    dst_ref=received.at[chunk, step - 1],
                    send_sem=send_sem.at[chunk, step - 1],
                    recv_sem=recv_sem.at[chunk, step - 1],
                    device_id=peer(axis, place),
                    device_id_type=MESH,
                )
                copy.start()
                copies.append(copy)
            waiting.extend(copies)
            return copies

        def end(axis, chunk, copies):
            received, summed = refs(axis)[:2]
            mine = coords[axis]
            if axis == "c":
                value = held[mine, chunk]
            else:
                value = refs("cyz"["cyz".index(axis) - 1])[1][chunk, mine]
            for step, copy in enumerate(copies):
                copy.wait_recv()
                value = value + received[chunk, step]
            summed[chunk] = value

        flights = {}
        for chunk in range(2):
            pack(chunk)
            flights["c", chunk] = begin("c", chunk)
        pass_on(2)
        input_terms(1, True)
        for chunk in range(2):
            end("c", chunk, flights["c", chunk])
            flights["y", chunk] = begin("y", chunk)
        near_input()
        for chunk in range(2):
            end("y", chunk, flights["y", chunk])
            flights["z", chunk] = begin("z", chunk)
        far_input()
        for chunk in range(2):
            end("z", chunk, flights["z", chunk])
        received, _, send_sem, recv_sem = refs("x")
        kept = refs("z")[1]
        copy = pltpu.make_async_remote_copy(
            src_ref=kept.at[1 - side],
            dst_ref=received,
            send_sem=send_sem,
            recv_sem=recv_sem,
            device_id=peer("x", 1 - side),
            device_id_type=MESH,
        )
        copy.start()
        waiting.append(copy)
        copy.wait_recv()
        weight_grad_ref[...] = kept[side] + received[...]
    else:
        pass_on(2)
        input_terms(1, True)
        near_input()
        far_input()
        weight_grad_ref[...] = partial[...]

    for copy in waiting:
        copy.wait_send()

    @pl.when(passes)
    def _():
        for index in range(3):
            passed(index).wait_send()


def fused_device(pre_act, grad_out, weight):
    samples, channels, local_x, rows, lanes = pre_act.shape
    out_chan, taps = grad_out.shape[1], weight.shape[0]
    space_count, batch_count = lax.axis_size("space"), lax.axis_size("batch")
    fits = (
        samples == 1
        and local_x == 1
        and taps == 27
        and rows == 8
        and lanes == 128
        and out_chan == 128
        and channels % 16 == 0
        and space_count % 2 == 0
    )
    if not fits:
        return on_device(pre_act, grad_out, weight)
    count = samples * batch_count * local_x * space_count * rows * lanes
    factor = 1.0 / count**0.5
    devices = space_count * batch_count
    total_rows = taps * channels
    scatter = (
        space_count > 2 and batch_count % 2 == 0 and batch_count > 2 and total_rows % devices == 0
    )
    cells = rows * lanes
    widest = max(channels, out_chan)
    bf16, f32 = jnp.bfloat16, jnp.float32
    scratch = [
        pltpu.VMEM((channels, rows, lanes), bf16),
        pltpu.VMEM((out_chan, rows, lanes), bf16),
        pltpu.VMEM((taps, channels, out_chan), bf16),
        pltpu.VMEM((2, channels, rows, lanes), bf16),
        pltpu.VMEM((2, out_chan, rows, lanes), bf16),
        pltpu.VMEM((widest * rows, lanes), f32),
        pltpu.VMEM((3, 3 * channels, cells + 2 * lanes), bf16),
        pltpu.VMEM((3, 3 * out_chan, cells + 2 * lanes), bf16),
        pltpu.VMEM((channels, cells), f32),
        pltpu.VMEM((total_rows + 8 if scatter else total_rows, out_chan), f32),
        *[pltpu.SemaphoreType.DMA((3,))] * 5,
    ]
    owned = total_rows
    if scatter:
        piece = total_rows // devices
        owned = -(-piece // 8) * 8
        sizes = [space_count // 2, batch_count // 2]
        tile = (owned, out_chan)
        scratch.append(pltpu.VMEM((2, 2, *sizes, *tile), f32))
        for number, extent in enumerate([2, *sizes]):
            rest = (*sizes[number:], *tile)
            scratch += [
                pltpu.VMEM((2, extent - 1, *rest), f32),
                pltpu.VMEM((2, *rest), f32),
                pltpu.SemaphoreType.DMA((2, extent - 1)),
                pltpu.SemaphoreType.DMA((2, extent - 1)),
            ]
        scratch += [
            pltpu.VMEM(tile, f32),
            pltpu.VMEM(tile, f32),
            pltpu.SemaphoreType.DMA,
            pltpu.SemaphoreType.DMA,
        ]
    vmem = pl.BlockSpec(memory_space=pltpu.VMEM)
    grad_in, weight_grad = pl.pallas_call(
        functools.partial(kernel, (space_count, batch_count), factor, scatter),
        out_shape=(
            jax.ShapeDtypeStruct((channels, rows, lanes), bf16),
            jax.ShapeDtypeStruct((owned, out_chan), f32),
        ),
        in_specs=[pl.BlockSpec(memory_space=pltpu.HBM)] * 3,
        out_specs=(vmem, vmem),
        scratch_shapes=scratch,
        compiler_params=pltpu.CompilerParams(
            collective_id=0, has_side_effects=True, vmem_limit_bytes=67043328
        ),
    )(
        pre_act.reshape(channels, rows, lanes),
        grad_out.reshape(out_chan, rows, lanes),
        weight,
    )
    grad_in = grad_in.reshape(pre_act.shape)
    if scatter:
        return grad_in, weight_grad[:piece].reshape(-1)
    space_part = lax.psum_scatter(
        weight_grad.reshape(-1), "space", scatter_dimension=0, tiled=True
    )
    return grad_in, lax.psum_scatter(space_part, "batch", scatter_dimension=0, tiled=True)


def solution(mesh):
    return jax.shard_map(
        fused_device,
        mesh=mesh,
        in_specs=(
            P("batch", None, "space", None, None),
            P("batch", None, "space", None, None),
            P(),
        ),
        out_specs=(P("batch", None, "space", None, None), P(("space", "batch"))),
        check_vma=False,
    )
```

time: 40.1 us -> 36.8 us (0.918)
  Pallas kernels: 35.1 us -> 33 us
  local copies, waits for them, and re-layouts: 4.13 us -> 2.93 us
    pallas_call x1, Pallas kernels: 35.1 us -> 33 us  [fused_device(): pl.pallas_call(functools.partial(kernel, (space_count, batch_count), fact...]
    unnamed x7 -> x1, local copies, waits for them, and re-layouts: 3.51 us -> 1.57 us
    reshape x1, local copies, waits for them, and re-layouts: 0.61 us -> 1.36 us  [fused_device(): return (grad_in, weight_grad[:piece].reshape(-1))]
where the time goes in v2:
time: 36.8 us; the launch traced here: 36.6 us
  Pallas kernels  33 us (90%)
  local copies, waits for them, and re-layouts  2.93 us (8%)
  between operations  0.64 us (2%)
    pallas_call x1, Pallas kernels, fused_device(): pl.pallas_call(functools.partial(kernel, (space_count, batch_count), fact...  33 us
    unnamed x1, local copies, waits for them, and re-layouts  1.57 us
    reshape x1, local copies, waits for them, and re-layouts, fused_device(): return (grad_in, weight_grad[:piece].reshape(-1))  1.36 us

profile of v2, /device:TPU:0, one launch (start us, length us, event | category | flops | bytes accessed | tf_op | source)
XLA Modules:
  0.0 36.6 jit_solution(10799573126733498034)
XLA Ops:
  0.6 33.0 %shard_map.50 = (bf16[64,8,128]{2,1,0:T(8,128)(2,1)}, f32[56,128]{1,0:T(8,128)}) custom-call(bf16[64,8,128]{2,1,0:T(8,128)(2,1)} %bitcast.8, bf16[128,8,128]{2,1,0:T(8,128)(2,1)} %bitcast.7, bf16[27,64,128]{2,1,0:T(8,128)(2,1)} %weight_hbm.1), custom_call_target="tpu_custom_call" | custom-call | tf_op jit(solution)/shard_map/pallas_call | solution.py:458
  33.7 1.4 %slice_bitcast_fusion = f32[6912]{0:T(1024)} fusion(f32[56,128]{1,0:T(8,128)} %get-tuple-element.5), kind=kLoop, calls=%fused_computation | loop fusion | bytes 55296 | tf_op jit(solution)/shard_map/reshape | solution.py:477
  35.0 1.6 %copy.7 = bf16[1,64,1,8,128]{4,3,2,1,0:T(8,128)(2,1)} copy(bf16[1,64,1,8,128]{4,3,2,1,0:T(8,128)(2,1)} %bitcast.9) | data formatting | bytes 262144

commit v3 on v2

--- a/solution.py
+++ b/solution.py
@@ -299,35 +299,37 @@
 
     waiting = list(sent)
     if scatter:
-        held, stages = stage_refs[0], stage_refs[1:]
-        padded_piece = held.shape[-2]
         piece = (partial.shape[0] - 8) // (space_count * batch_count)
         partial[partial.shape[0] - 8 :, :] = jnp.zeros((8, lanes), jnp.float32)
-
-        def pack(chunk):
-            for y in range(extents["y"]):
+        per_chunk = len(stage_refs) // 2
+        chunks, first_row = [], 0
+        for number, order in enumerate(("cxyz", "cyxz")):
+            refs = stage_refs[number * per_chunk : (number + 1) * per_chunk]
+            chunks.append((order, refs[0], refs[1:], first_row, refs[0].shape[-2]))
+            first_row += refs[0].shape[-2]
+
+        def pack(order, held, first_row, count):
+            for s in range(space_count):
                 for b in range(batch_count):
-                    start = ((2 * y + chunk) * batch_count + b) * piece
-                    held[b % 2, chunk, y, b // 2] = partial[start : start + padded_piece, :]
-
-        def refs(axis):
-            number = "cyzx".index(axis)
-            return stages[4 * number : 4 * number + 4]
-
-        def begin(axis, chunk):
-            received, _, send_sem, recv_sem = refs(axis)
+                    start = (s * batch_count + b) * piece + first_row
+                    place = dict(c=b % 2, z=b // 2, x=s % 2, y=s // 2)
+                    index = tuple(place[axis] for axis in order)
+                    held[index] = partial[start : start + count, :]
+
+        def source_of(chunk, number):
+            return chunk[1] if number == 0 else chunk[2][4 * number - 3]
+
+        def begin(chunk, number):
+            axis = chunk[0][number]
+            received, _, send_sem, recv_sem = chunk[2][4 * number : 4 * number + 4]
             copies = []
             for step in range(1, extents[axis]):
                 place = lax.rem(coords[axis] + step, extents[axis])
-                if axis == "c":
-                    source = held.at[place, chunk]
-                else:
-                    source = refs("cyz"["cyz".index(axis) - 1])[1].at[chunk, place]
                 copy = pltpu.make_async_remote_copy(
-                    src_ref=source,
-                    dst_ref=received.at[chunk, step - 1],
-                    send_sem=send_sem.at[chunk, step - 1],
-                    recv_sem=recv_sem.at[chunk, step - 1],
+                    src_ref=source_of(chunk, number).at[place],
+                    dst_ref=received.at[step - 1],
+                    send_sem=send_sem.at[step - 1],
+                    recv_sem=recv_sem.at[step - 1],
                     device_id=peer(axis, place),
                     device_id_type=MESH,
                 )
@@ -336,48 +338,34 @@
             waiting.extend(copies)
             return copies
 
-        def end(axis, chunk, copies):
-            received, summed = refs(axis)[:2]
-            mine = coords[axis]
-            if axis == "c":
-                value = held[mine, chunk]
-            else:
-                value = refs("cyz"["cyz".index(axis) - 1])[1][chunk, mine]
+        def end(chunk, number, copies):
+            received, summed = chunk[2][4 * number : 4 * number + 2]
+            value = source_of(chunk, number)[coords[chunk[0][number]]]
             for step, copy in enumerate(copies):
                 copy.wait_recv()
-                value = value + received[chunk, step]
-            summed[chunk] = value
-
-        flights = {}
-        for chunk in range(2):
-            pack(chunk)
-            flights["c", chunk] = begin("c", chunk)
+                value = value + received[step]
+            if number < 3:
+                summed[...] = value
+            else:
+                weight_grad_ref[chunk[3] : chunk[3] + chunk[4], :] = value
+
+        flights = []
+        for chunk in chunks:
+            pack(chunk[0], chunk[1], chunk[3], chunk[4])
+            flights.append(begin(chunk, 0))
         pass_on(2)
-        input_terms(1, True)
-        for chunk in range(2):
-            end("c", chunk, flights["c", chunk])
-            flights["y", chunk] = begin("y", chunk)
-        near_input()
-        for chunk in range(2):
-            end("y", chunk, flights["y", chunk])
-            flights["z", chunk] = begin("z", chunk)
-        far_input()
-        for chunk in range(2):
-            end("z", chunk, flights["z", chunk])
-        received, _, send_sem, recv_sem = refs("x")
-        kept = refs("z")[1]
-        copy = pltpu.make_async_remote_copy(
-            src_ref=kept.at[1 - side],
-            dst_ref=received,
-            send_sem=send_sem,
-            recv_sem=recv_sem,
-            device_id=peer("x", 1 - side),
-            device_id_type=MESH,
-        )
-        copy.start()
-        waiting.append(copy)
-        copy.wait_recv()
-        weight_grad_ref[...] = kept[side] + received[...]
+        for number in range(1, 4):
+            for place, chunk in enumerate(chunks):
+                end(chunk, number - 1, flights[place])
+                flights[place] = begin(chunk, number)
+            if number == 1:
+                input_terms(1, True)
+            elif number == 2:
+                near_input()
+            else:
+                far_input()
+        for place, chunk in enumerate(chunks):
+            end(chunk, 3, flights[place])
     else:
         pass_on(2)
         input_terms(1, True)
@@ -416,6 +404,7 @@
     total_rows = taps * channels
     scatter = (
         space_count > 2 and batch_count % 2 == 0 and batch_count > 2 and total_rows % devices == 0
+        and total_rows // devices > 8
     )
     cells = rows * lanes
     widest = max(channels, out_chan)
@@ -437,23 +426,19 @@
     if scatter:
         piece = total_rows // devices
         owned = -(-piece // 8) * 8
-        sizes = [space_count // 2, batch_count // 2]
-        tile = (owned, out_chan)
-        scratch.append(pltpu.VMEM((2, 2, *sizes, *tile), f32))
-        for number, extent in enumerate([2, *sizes]):
-            rest = (*sizes[number:], *tile)
-            scratch += [
-                pltpu.VMEM((2, extent - 1, *rest), f32),
-                pltpu.VMEM((2, *rest), f32),
-                pltpu.SemaphoreType.DMA((2, extent - 1)),
-                pltpu.SemaphoreType.DMA((2, extent - 1)),
-            ]
-        scratch += [
-            pltpu.VMEM(tile, f32),
-            pltpu.VMEM(tile, f32),
-            pltpu.SemaphoreType.DMA,
-            pltpu.SemaphoreType.DMA,
-        ]
+        extents = dict(c=2, x=2, y=space_count // 2, z=batch_count // 2)
+        upper = -(-owned // 16) * 8
+        for order, count in (("cxyz", upper), ("cyxz", owned - upper)):
+            sizes = [extents[axis] for axis in order]
+            scratch.append(pltpu.VMEM((*sizes, count, out_chan), f32))
+            for number, extent in enumerate(sizes):
+                rest = (*sizes[number + 1 :], count, out_chan)
+                scratch += [
+                    pltpu.VMEM((extent - 1, *rest), f32),
+                    pltpu.VMEM(rest, f32),
+                    pltpu.SemaphoreType.DMA((extent - 1,)),
+                    pltpu.SemaphoreType.DMA((extent - 1,)),
+                ]
     vmem = pl.BlockSpec(memory_space=pltpu.VMEM)
     grad_in, weight_grad = pl.pallas_call(
         functools.partial(kernel, (space_count, batch_count), factor, scatter),
@@ -465,12 +450,12 @@
         out_specs=(vmem, vmem),
         scratch_shapes=scratch,
         compiler_params=pltpu.CompilerParams(
-            collective_id=0, has_side_effects=True, vmem_limit_bytes=67043328
+            collective_id=0, has_side_effects=True, vmem_limit_bytes=48 * 2**20
         ),
     )(
-        pre_act.reshape(channels, rows, lanes),
-        grad_out.reshape(out_chan, rows, lanes),
-        weight,
+        pltpu.with_memory_space_constraint(pre_act.reshape(channels, rows, lanes), pltpu.HBM),
+        pltpu.with_memory_space_constraint(grad_out.reshape(out_chan, rows, lanes), pltpu.HBM),
+        pltpu.with_memory_space_constraint(weight, pltpu.HBM),
     )
     grad_in = grad_in.reshape(pre_act.shape)
     if scatter:

time: 36.8 us -> 31.6 us (0.86)
  Pallas kernels: 33 us -> 29.5 us
  local copies, waits for them, and re-layouts: 2.93 us -> 1.27 us
    pallas_call x1, Pallas kernels: 33 us -> 29.5 us  [fused_device(): pl.pallas_call(functools.partial(kernel, (space_count, batch_count), fact...]
    unnamed x1, local copies, waits for them, and re-layouts: 1.57 us -> 0.65 us
    reshape x1, local copies, waits for them, and re-layouts: 1.36 us -> 0.61 us  [fused_device(): return (grad_in, weight_grad[:piece].reshape(-1))]
where the time goes in v3:
time: 31.6 us; the launch traced here: 31.4 us
  Pallas kernels  29.5 us (93%)
  local copies, waits for them, and re-layouts  1.27 us (4%)
  between operations  0.64 us (2%)
    pallas_call x1, Pallas kernels, fused_device(): pl.pallas_call(functools.partial(kernel, (space_count, batch_count), fact...  29.5 us
    unnamed x1, local copies, waits for them, and re-layouts  0.65 us

profile of v3, /device:TPU:0, one launch (start us, length us, event | category | flops | bytes accessed | tf_op | source)
XLA Modules:
  0.0 31.4 jit_solution(12000612536530402328)
XLA Ops:
  0.6 29.5 %shard_map.50 = (bf16[64,8,128]{2,1,0:T(8,128)(2,1)S(1)}, f32[56,128]{1,0:T(8,128)S(1)}) custom-call(bf16[64,8,128]{2,1,0:T(8,128)(2,1)} %bitcast.9, bf16[128,8,128]{2,1,0:T(8,128)(2,1)} %bitcast.8, bf16[27,64,128]{2,1,0:T(8,128)(2,1)} %weight_hbm.1), custom_call_target="tpu_custom_call" | custom-call | tf_op jit(solution)/shard_map/pallas_call | solution.py:443
  30.2 0.6 %slice_bitcast_fusion = f32[6912]{0:T(1024)} fusion(f32[56,128]{1,0:T(8,128)S(1)} %get-tuple-element.5), kind=kLoop, calls=%fused_computation | loop fusion | bytes 55296 | tf_op jit(solution)/shard_map/reshape | solution.py:462
  30.8 0.7 %copy.7 = bf16[1,64,1,8,128]{4,3,2,1,0:T(8,128)(2,1)} copy(bf16[1,64,1,8,128]{4,3,2,1,0:T(8,128)(2,1)S(1)} %bitcast.7) | data formatting | bytes 262144

commit v4 on v3

--- a/solution.py
+++ b/solution.py
@@ -105,7 +105,7 @@
 def kernel(
     sizes,
     factor,
-    scatter,
+    orders,
     pre_hbm,
     grad_hbm,
     weight_hbm,
@@ -153,7 +153,7 @@
 
     barrier = pltpu.get_barrier_semaphore()
     low, high = space >= 2, space < space_count - 2
-    if scatter:
+    if orders:
         greeted = 0
         for axis, extent in extents.items():
             for step in range(1, extent):
@@ -177,9 +177,10 @@
 
         pl.semaphore_wait(barrier, 1 + jnp.where(low, 1, 0) + jnp.where(high, 1, 0))
 
-    half = out_chan // 2
+    half, quarter = out_chan // 2, channels // 2
     messages = [
-        (pre_hbm, lambda slot: pre_halo.at[slot]),
+        (pre_hbm.at[0:quarter], lambda slot: pre_halo.at[slot, 0:quarter]),
+        (pre_hbm.at[quarter:channels], lambda slot: pre_halo.at[slot, quarter:channels]),
         (grad_hbm.at[0:half], lambda slot: grad_halo.at[slot, 0:half]),
         (grad_hbm.at[half:out_chan], lambda slot: grad_halo.at[slot, half:out_chan]),
     ]
@@ -210,7 +211,7 @@
             device_id_type=MESH,
         )
 
-    sent = [direct(index) for index in range(3)]
+    sent = [direct(index) for index in range(4)]
     for copy in sent:
         copy.start()
 
@@ -221,10 +222,11 @@
         def _():
             passed(index).start()
 
-    def take(index, target):
+    def take(first, target):
         @pl.when(gets)
         def _():
-            passed(index).wait_recv()
+            passed(first).wait_recv()
+            passed(first + 1).wait_recv()
 
         @pl.when(jnp.logical_not(gets))
         def _():
@@ -270,11 +272,11 @@
     grad_plane(grad_ref[...], 1)
     hidden_plane(pre_ref[...], 1)
     pass_on(0)
+    pass_on(1)
     weight_terms(1)
     hidden_plane(pre_halo[near], near_place)
     weight_terms(near_place)
     local[2].wait()
-    pass_on(1)
     take(0, pre_halo)
     hidden_plane(pre_halo[side], far_place)
     weight_terms(far_place)
@@ -284,10 +286,6 @@
         input_terms(near_place, False)
 
     def far_input():
-        @pl.when(gets)
-        def _():
-            passed(1).wait_recv()
-
         take(2, grad_halo)
         grad_plane(grad_halo[side], far_place)
         input_terms(far_place, False)
@@ -298,12 +296,12 @@
         grad_in_ref[...] = (back * jnp.where(act > 0, 1.0, slope)).astype(grad_in_ref.dtype)
 
     waiting = list(sent)
-    if scatter:
+    if orders:
         piece = (partial.shape[0] - 8) // (space_count * batch_count)
         partial[partial.shape[0] - 8 :, :] = jnp.zeros((8, lanes), jnp.float32)
-        per_chunk = len(stage_refs) // 2
+        per_chunk = len(stage_refs) // len(orders)
         chunks, first_row = [], 0
-        for number, order in enumerate(("cxyz", "cyxz")):
+        for number, order in enumerate(orders):
             refs = stage_refs[number * per_chunk : (number + 1) * per_chunk]
             chunks.append((order, refs[0], refs[1:], first_row, refs[0].shape[-2]))
             first_row += refs[0].shape[-2]
@@ -361,6 +359,7 @@
             if number == 1:
                 input_terms(1, True)
             elif number == 2:
+                pass_on(3)
                 near_input()
             else:
                 far_input()
@@ -368,6 +367,7 @@
             end(chunk, 3, flights[place])
     else:
         pass_on(2)
+        pass_on(3)
         input_terms(1, True)
         near_input()
         far_input()
@@ -378,7 +378,7 @@
 
     @pl.when(passes)
     def _():
-        for index in range(3):
+        for index in range(4):
             passed(index).wait_send()
 
 
@@ -420,15 +420,17 @@
         pltpu.VMEM((3, 3 * out_chan, cells + 2 * lanes), bf16),
         pltpu.VMEM((channels, cells), f32),
         pltpu.VMEM((total_rows + 8 if scatter else total_rows, out_chan), f32),
-        *[pltpu.SemaphoreType.DMA((3,))] * 5,
+        *[pltpu.SemaphoreType.DMA((4,))] * 5,
     ]
-    owned = total_rows
+    owned, orders = total_rows, ()
     if scatter:
         piece = total_rows // devices
         owned = -(-piece // 8) * 8
         extents = dict(c=2, x=2, y=space_count // 2, z=batch_count // 2)
-        upper = -(-owned // 16) * 8
-        for order, count in (("cxyz", upper), ("cyxz", owned - upper)):
+        tiles = owned // 8
+        orders = ("cxyz", "cyxz") * min(2, tiles // 2)
+        shares = [tiles // len(orders) + (n < tiles % len(orders)) for n in range(len(orders))]
+        for order, count in zip(orders, [8 * share for share in shares]):
             sizes = [extents[axis] for axis in order]
             scratch.append(pltpu.VMEM((*sizes, count, out_chan), f32))
             for number, extent in enumerate(sizes):
@@ -441,7 +443,7 @@
                 ]
     vmem = pl.BlockSpec(memory_space=pltpu.VMEM)
     grad_in, weight_grad = pl.pallas_call(
-        functools.partial(kernel, (space_count, batch_count), factor, scatter),
+        functools.partial(kernel, (space_count, batch_count), factor, orders),
         out_shape=(
             jax.ShapeDtypeStruct((channels, rows, lanes), bf16),
             jax.ShapeDtypeStruct((owned, out_chan), f32),

time: 31.6 us -> 29 us (0.918)
  Pallas kernels: 29.5 us -> 26.9 us
    pallas_call x1, Pallas kernels: 29.5 us -> 26.9 us  [fused_device(): pl.pallas_call(functools.partial(kernel, (space_count, batch_count), fact...]
where the time goes in v4:
time: 29 us; the launch traced here: 28.8 us
  Pallas kernels  26.9 us (93%)
  local copies, waits for them, and re-layouts  1.27 us (4%)
  between operations  0.64 us (2%)
    pallas_call x1, Pallas kernels, fused_device(): pl.pallas_call(functools.partial(kernel, (space_count, batch_count), fact...  26.9 us
    unnamed x1, local copies, waits for them, and re-layouts  0.65 us
    reshape x1, local copies, waits for them, and re-layouts, fused_device(): return (grad_in, weight_grad[:piece].reshape(-1))  0.61 us

profile of v4, /device:TPU:0, one launch (start us, length us, event | category | flops | bytes accessed | tf_op | source)
XLA Modules:
  0.0 28.8 jit_solution(8189810414532574649)
XLA Ops:
  0.6 26.9 %shard_map.50 = (bf16[64,8,128]{2,1,0:T(8,128)(2,1)S(1)}, f32[56,128]{1,0:T(8,128)S(1)}) custom-call(bf16[64,8,128]{2,1,0:T(8,128)(2,1)} %bitcast.9, bf16[128,8,128]{2,1,0:T(8,128)(2,1)} %bitcast.8, bf16[27,64,128]{2,1,0:T(8,128)(2,1)} %weight_hbm.1), custom_call_target="tpu_custom_call" | custom-call | tf_op jit(solution)/shard_map/pallas_call | solution.py:445
  27.6 0.6 %slice_bitcast_fusion = f32[6912]{0:T(1024)} fusion(f32[56,128]{1,0:T(8,128)S(1)} %get-tuple-element.5), kind=kLoop, calls=%fused_computation | loop fusion | bytes 55296 | tf_op jit(solution)/shard_map/reshape | solution.py:464
  28.2 0.7 %copy.7 = bf16[1,64,1,8,128]{4,3,2,1,0:T(8,128)(2,1)} copy(bf16[1,64,1,8,128]{4,3,2,1,0:T(8,128)(2,1)S(1)} %bitcast.7) | data formatting | bytes 262144

commit v5 on v4

--- a/solution.py
+++ b/solution.py
@@ -351,12 +351,12 @@
         for chunk in chunks:
             pack(chunk[0], chunk[1], chunk[3], chunk[4])
             flights.append(begin(chunk, 0))
-        pass_on(2)
         for number in range(1, 4):
             for place, chunk in enumerate(chunks):
                 end(chunk, number - 1, flights[place])
                 flights[place] = begin(chunk, number)
             if number == 1:
+                pass_on(2)
                 input_terms(1, True)
             elif number == 2:
                 pass_on(3)

time: 29 us -> 28.2 us (0.972)
  Pallas kernels: 26.9 us -> 25.8 us
    pallas_call x1, Pallas kernels: 26.9 us -> 25.8 us  [fused_device(): pl.pallas_call(functools.partial(kernel, (space_count, batch_count), fact...]
where the time goes in v5:
time: 28.2 us; the launch traced here: 27.7 us
  Pallas kernels  25.8 us (91%)
  local copies, waits for them, and re-layouts  1.27 us (5%)
  between operations  0.64 us (2%)
    pallas_call x1, Pallas kernels, fused_device(): pl.pallas_call(functools.partial(kernel, (space_count, batch_count), fact...  25.8 us
    unnamed x1, local copies, waits for them, and re-layouts  0.65 us
    reshape x1, local copies, waits for them, and re-layouts, fused_device(): return (grad_in, weight_grad[:piece].reshape(-1))  0.61 us

profile of v5, /device:TPU:0, one launch (start us, length us, event | category | flops | bytes accessed | tf_op | source)
XLA Modules:
  0.0 27.7 jit_solution(4233686201808651723)
XLA Ops:
  0.6 25.8 %shard_map.50 = (bf16[64,8,128]{2,1,0:T(8,128)(2,1)S(1)}, f32[56,128]{1,0:T(8,128)S(1)}) custom-call(bf16[64,8,128]{2,1,0:T(8,128)(2,1)} %bitcast.9, bf16[128,8,128]{2,1,0:T(8,128)(2,1)} %bitcast.8, bf16[27,64,128]{2,1,0:T(8,128)(2,1)} %weight_hbm.1), custom_call_target="tpu_custom_call" | custom-call | tf_op jit(solution)/shard_map/pallas_call | solution.py:445
  26.5 0.6 %slice_bitcast_fusion = f32[6912]{0:T(1024)} fusion(f32[56,128]{1,0:T(8,128)S(1)} %get-tuple-element.5), kind=kLoop, calls=%fused_computation | loop fusion | bytes 55296 | tf_op jit(solution)/shard_map/reshape | solution.py:464
  27.1 0.7 %copy.7 = bf16[1,64,1,8,128]{4,3,2,1,0:T(8,128)(2,1)} copy(bf16[1,64,1,8,128]{4,3,2,1,0:T(8,128)(2,1)S(1)} %bitcast.7) | data formatting | bytes 262144
